TPU v7x, 32 devices: a whole 2x2x4 slice. The times are simulated.
32 devices in a mesh: seq: 4 (over y, x), head: 8 (over z, core).
Axes of the slice: x: 2, y: 2, z: 4, core: 2. Of those that a mesh axis runs over, the one named last changes fastest.
Arguments:
- inputs: bfloat16 [4096, 6144], P('seq', 'head'), may hold values from -6 to 6
- projection: bfloat16 [6144, 3, 4096], P('seq', None, 'head'), may hold values from -0.078125 to 0.078125
- cotangent: bfloat16 [4096, 4096], P('seq', 'head'), may hold values from -0.3125 to 0.3125
- log_decay: float32 [32, 4096], P('head', 'seq'), may hold values from -0.7 to 0
- document_starts: int32 [4], replicated, may hold values from 0 to 3328, as said below
Outputs:
- input_gradient: bfloat16 [4096, 6144], P('seq', 'head')
- weight_gradient: bfloat16 [6144, 3, 4096], P('seq', None, 'head')
Inputs may be any that keep to these rules, and one draw needn't show every extreme that they name: `document_starts`: strictly increasing; the first is 0 and the last is (3) * 1024 + 256.
All inputs are finite; a program needn't handle non-finite values.
Results may differ from a plain program's by a relative error of at most 0.02.
Values may be sent and summed in bfloat16 or wider, within the bound.
A program may use at most 192 MiB of HBM per device.

v0:
```python
import jax
import jax.numpy as jnp
from jax import lax
from jax.sharding import PartitionSpec as P

HEAD_DIM = 128
BLOCK = 256


def hop(array, axis, flip):
    return lax.ppermute(array, axis, [(i, i ^ flip) for i in range(lax.axis_size(axis))])


def gather_states(packed, axis):
    length = lax.axis_size(axis)
    if length != 4:
        return lax.all_gather(packed, axis)
    place = lax.axis_index(axis)
    parts = [packed] + [hop(packed, axis, flip) for flip in range(1, length)]
    rows = []
    for at in range(length):
        row = parts[0]
        for flip in range(1, length):
            row = jnp.where(place == at ^ flip, parts[flip], row)
        rows.append(row)
    return rows


def combine_devices(states, decays, place, reverse):
    length = len(decays)
    total = jnp.zeros_like(states[0])
    for k in range(length):
        at = length - 1 - k if reverse else k
        reached = at > place if reverse else at < place
        total = jnp.where(reached, decays[at][:, None, None] * total + states[at], total)
    return total


def gather_rows(part, axis):
    length, place, rows = (lax.axis_size(axis), lax.axis_index(axis), part.shape[1])
    if length != 4:
        whole = lax.all_gather(part, axis, axis=1, tiled=True)
        return [(0, 0, whole)]
    half = rows // 2
    low, high = (part[:, :half], part[:, half:])
    x_high = hop(high, axis, 1)
    y_low = hop(low, axis, 2)
    x_low = hop(low, axis, 1)
    y_high = hop(high, axis, 2)
    d_low = hop(y_low, axis, 1)
    d_high = hop(x_high, axis, 2)
    return [
        (place, 0, low),
        (place, half, high),
        (place ^ 1, half, x_high),
        (place ^ 2, 0, y_low),
        (place ^ 1, 0, x_low),
        (place ^ 2, half, y_high),
        (place ^ 3, 0, d_low),
        (place ^ 3, half, d_high),
    ]


def scatter_rows(partial, axis, rows):
    length, place = (lax.axis_size(axis), lax.axis_index(axis))
    if length != 4:
        return lax.psum_scatter(partial(0, 0, rows * length), axis, scatter_dimension=1, tiled=True)
    half = rows // 2

    def add(*terms):
        return sum((term.astype(jnp.float32) for term in terms)).astype(jnp.bfloat16)

    far_low = hop(partial(place ^ 3, 0, half), axis, 1)
    far_high = hop(partial(place ^ 3, half, half), axis, 2)
    x_low = hop(partial(place ^ 1, 0, half), axis, 1)
    y_high = hop(partial(place ^ 2, half, half), axis, 2)
    x_high = hop(add(partial(place ^ 1, half, half), far_high), axis, 1)
    y_low = hop(add(partial(place ^ 2, 0, half), far_low), axis, 2)
    own_low, own_high = (partial(place, 0, half), partial(place, half, half))
    return jnp.concatenate([add(own_low, x_low, y_low), add(own_high, x_high, y_high)], axis=1)


def silu_slope(point):
    sigma = jax.nn.sigmoid(point)
    return sigma * (1.0 + point * (1.0 - sigma))


def block_factors(decay_sum, doc_index, doc_begin):
    inside = jnp.arange(doc_index.shape[-1], dtype=jnp.int32)
    causal = inside[:, None] >= inside[None, :]
    same_doc = (doc_index[:, :, None] == doc_index[:, None, :]) & causal[None]
    spread = jnp.minimum(decay_sum[..., :, None] - decay_sum[..., None, :], 0.0)
    pair_weight = jnp.where(same_doc[None], jnp.exp(spread), 0.0)
    to_end = jnp.where(
        (doc_index == doc_index[:, -1:])[None], jnp.exp(decay_sum[..., -1:] - decay_sum), 0.0
    )
    began_flag = doc_index == doc_index[:, :1] - doc_begin[:, :1]
    from_start = jnp.where(began_flag[None], jnp.exp(decay_sum), 0.0)
    return (pair_weight, to_end, from_start, from_start[..., -1])


def block_pair(decay):
    high = decay.astype(jnp.bfloat16)
    low = (decay - high.astype(jnp.float32)).astype(jnp.bfloat16)
    pair = jnp.stack([high, low], axis=1)
    slab = jnp.pad(pair, ((0, HEAD_DIM - pair.shape[0]), (0, HEAD_DIM - 2)))
    return slab[None]


def combine_states(earlier, later):
    return (earlier[0] * later[0], later[0][:, None, None] * earlier[1] + later[1])


def body(inputs, projection, cotangent, log_decay, document_starts):
    tokens = inputs.shape[0]
    heads_here = log_decay.shape[0]
    local_cols = cotangent.shape[1]
    blocks = tokens // BLOCK
    query_scale = HEAD_DIM ** (-0.5)
    features = lax.all_gather(inputs, "head", axis=1, tiled=True)
    rows = projection.shape[0]
    blocks_w = gather_rows(projection.transpose(1, 0, 2), "seq")

    def feature_rows(owner, first, count):
        return lax.dynamic_slice_in_dim(features, owner * rows + first, count, axis=1)

    projected = sum(
        (
            jnp.einsum(
                "td,kdc->ktc",
                feature_rows(owner, first, block.shape[1]),
                block,
                preferred_element_type=jnp.float32,
            )
            for owner, first, block in blocks_w
        )
    )
    queries = (jax.nn.silu(projected[0]) * query_scale).astype(jnp.bfloat16)
    keys = jax.nn.silu(projected[1]).astype(jnp.bfloat16)
    values = projected[2].astype(jnp.bfloat16)

    def split_blocks(table):
        return table.reshape(blocks, BLOCK, heads_here, HEAD_DIM).transpose(2, 0, 1, 3)

    def merge_blocks(table):
        return table.transpose(1, 2, 0, 3).reshape(tokens, local_cols)

    queries_b = split_blocks(queries)
    keys_b = split_blocks(keys)
    values_b = split_blocks(values)
    upstream = split_blocks(cotangent)
    offset = lax.axis_index("seq") * tokens
    positions = offset + jnp.arange(tokens, dtype=jnp.int32)
    doc_index = (
        jnp.sum((document_starts[None, :] <= positions[:, None]).astype(jnp.int32), axis=1) - 1
    )
    doc_begin = jnp.any(document_starts[None, :] == positions[:, None], axis=1).astype(jnp.int32)
    decay_sum = jnp.cumsum(log_decay.reshape(heads_here, blocks, BLOCK), axis=-1)
    pair_weight, to_end, from_start, block_decay = block_factors(
        decay_sum, doc_index.reshape(blocks, BLOCK), doc_begin.reshape(blocks, BLOCK)
    )
    keys_weighted = (keys_b.astype(jnp.float32) * to_end[..., None]).astype(jnp.bfloat16)
    queries_weighted = (queries_b.astype(jnp.float32) * from_start[..., None]).astype(jnp.bfloat16)
    key_state = jnp.einsum(
        "hbse,hbsf->hbef", keys_weighted, values_b, preferred_element_type=jnp.float32
    )
    query_state = jnp.einsum(
        "hbte,hbtf->hbef", queries_weighted, upstream, preferred_element_type=jnp.float32
    )

    def local_step(carry, item):
        return (combine_states(carry, item), carry)

    ones = jnp.ones((heads_here,), jnp.float32)
    empty = jnp.zeros((heads_here, HEAD_DIM, HEAD_DIM), jnp.float32)
    (device_decay, device_keys), (prior_decay, prior_keys) = lax.scan(
        local_step, (ones, empty), (block_decay.T, key_state.swapaxes(0, 1))
    )
    (device_decay_back, device_query), (later_decay, later_query) = lax.scan(
        local_step, (ones, empty), (block_decay.T, query_state.swapaxes(0, 1)), reverse=True
    )
    place = lax.axis_index("seq")
    rough = block_pair(device_decay)
    packed = jnp.concatenate(
        [device_keys.astype(jnp.bfloat16), device_query.astype(jnp.bfloat16), rough]
    )
    everything = gather_states(packed, "seq")
    everything = [everything[k].astype(jnp.float32) for k in range(lax.axis_size("seq"))]
    decays = [
        part[2 * heads_here, :heads_here, 0] + part[2 * heads_here, :heads_here, 1]
        for part in everything
    ]
    forward_in = combine_devices([part[:heads_here] for part in everything], decays, place, False)
    backward_in = combine_devices(
        [part[heads_here : 2 * heads_here] for part in everything], decays, place, True
    )
    state_before = (
        (prior_decay[:, :, None, None] * forward_in[None] + prior_keys)
        .swapaxes(0, 1)
        .astype(jnp.bfloat16)
    )
    state_after = (
        (later_decay[:, :, None, None] * backward_in[None] + later_query)
        .swapaxes(0, 1)
        .astype(jnp.bfloat16)
    )
    query_key = (
        jnp.einsum("hbte,hbse->hbts", queries_b, keys_b, preferred_element_type=jnp.float32)
        * pair_weight
    ).astype(jnp.bfloat16)
    value_score = (
        jnp.einsum("hbtf,hbsf->hbts", upstream, values_b, preferred_element_type=jnp.float32)
        * pair_weight
    ).astype(jnp.bfloat16)
    query_gradient = jnp.einsum(
        "hbts,hbse->hbte", value_score, keys_b, preferred_element_type=jnp.float32
    ) + from_start[..., None] * jnp.einsum(
        "hbtf,hbef->hbte", upstream, state_before, preferred_element_type=jnp.float32
    )
    key_gradient = jnp.einsum(
        "hbts,hbte->hbse", value_score, queries_b, preferred_element_type=jnp.float32
    ) + to_end[..., None] * jnp.einsum(
        "hbsf,hbef->hbse", values_b, state_after, preferred_element_type=jnp.float32
    )
    value_gradient = jnp.einsum(
        "hbts,hbtf->hbsf", query_key, upstream, preferred_element_type=jnp.float32
    ) + to_end[..., None] * jnp.einsum(
        "hbse,hbef->hbsf", keys_b, state_after, preferred_element_type=jnp.float32
    )
    project_gradient = jnp.stack(
        [
            merge_blocks(query_gradient) * silu_slope(projected[0]) * query_scale,
            merge_blocks(key_gradient) * silu_slope(projected[1]),
            merge_blocks(value_gradient),
        ],
        axis=0,
    ).astype(jnp.bfloat16)

    def weight_partial(owner, first, count):
        return jnp.einsum(
            "td,ktc->kdc",
            feature_rows(owner, first, count),
            project_gradient,
            preferred_element_type=jnp.float32,
        ).astype(jnp.bfloat16)

    partial_value = jnp.zeros((tokens, features.shape[1]), jnp.bfloat16)
    for owner, first, block in blocks_w:
        piece = jnp.einsum(
            "ktc,kdc->td", project_gradient, block, preferred_element_type=jnp.float32
        ).astype(jnp.bfloat16)
        partial_value = lax.dynamic_update_slice_in_dim(
            partial_value, piece, owner * rows + first, axis=1
        )
    input_gradient = lax.psum_scatter(partial_value, "head", scatter_dimension=1, tiled=True)
    weight_gradient = scatter_rows(weight_partial, "seq", rows).transpose(1, 0, 2)
    return (input_gradient, weight_gradient)


def solution(mesh):
    placed = (P("seq", "head"), P("seq", None, "head"), P("seq", "head"), P("head", "seq"), P())
    return jax.shard_map(
        body,
        mesh=mesh,
        in_specs=placed,
        out_specs=(P("seq", "head"), P("seq", None, "head")),
        check_vma=False,
    )
```

profile of v0, /device:TPU:0, one launch (start us, length us, event | category | flops | bytes accessed | tf_op | source)
XLA Modules:
  0.0 527.8 jit_solution(1366227272367069007)
XLA Ops:
  27.3 41.3 %collective-permute-done.1 = bf16[3,768,512]{2,1,0:T(8,128)(2,1)} collective-permute-done((bf16[3,768,512]{2,1,0:T(8,128)(2,1)}, bf16[3,768,512]{2,1,0:T(8,128)(2,1)}, u32[]{:S(2)}, u32[]{:S(2)}) %collective-permute-start.1) | collective-permute-done | bytes 2359328 | tf_op jit(solution)/shard_map/ppermute | solution.py:11
  73.2 55.9 %all-gather.2.cloned.1.call-done = bf16[1024,6144]{1,0:T(8,128)(2,1)} async-done(((bf16[1024,768]{1,0:T(8,128)(2,1)}), bf16[1024,6144]{1,0:T(8,128)(2,1)}) %all-gather.2.cloned.1.call-update) | async-done | bytes 12582928 | tf_op jit(solution)/shard_map/all_gather | solution.py:120
  129.1 7.5 %fusion.43 = f32[1024,3,512]{2,0,1:T(8,128)} fusion(bf16[3,768,512]{2,1,0:T(8,128)(2,1)} %collective-permute-done, bf16[1024,6144]{1,0:T(8,128)(2,1)} %all-gather.2.cloned.1.call-done, s32[]{:T(128)S(6)} %select_n.169), kind=kOutput, calls=%fused_computation.81 | convolution fusion | flops 2415919104 | bytes 10223620 | tf_op jit(solution)/shard_map/td,kdc->ktc/dot_general | solution.py:129
  136.6 7.5 %fusion.40 = f32[1024,3,512]{2,0,1:T(8,128)} fusion(bf16[3,768,512]{2,1,0:T(8,128)(2,1)} %collective-permute-done.1, bf16[1024,6144]{1,0:T(8,128)(2,1)} %all-gather.2.cloned.1.call-done, s32[]{:T(128)S(6)} %select_n.170), kind=kOutput, calls=%fused_computation.78 | convolution fusion | flops 2415919104 | bytes 10223620 | tf_op jit(solution)/shard_map/td,kdc->ktc/dot_general | solution.py:129
  153.4 17.0 %collective-permute-done.4 = bf16[3,768,512]{2,1,0:T(8,128)(2,1)} collective-permute-done((bf16[3,768,512]{2,1,0:T(8,128)(2,1)}, bf16[3,768,512]{2,1,0:T(8,128)(2,1)}, u32[]{:S(2)}, u32[]{:S(2)}) %collective-permute-start.4) | collective-permute-done | bytes 2359328 | tf_op jit(solution)/shard_map/ppermute | solution.py:11
  170.4 6.1 %fusion.31 = f32[1024,3,512]{2,0,1:T(8,128)} fusion(bf16[3,768,512]{2,1,0:T(8,128)(2,1)} %collective-permute-done.4, bf16[1024,6144]{1,0:T(8,128)(2,1)S(1)} %bitcast.256, s32[]{:T(128)S(6)} %select_n.173), kind=kOutput, calls=%fused_computation.69 | convolution fusion | flops 2415919104 | bytes 10223620 | tf_op jit(solution)/shard_map/td,kdc->ktc/dot_general | solution.py:129
  176.6 6.2 %fusion.34 = f32[1024,3,512]{2,0,1:T(8,128)} fusion(bf16[3,768,512]{2,1,0:T(8,128)(2,1)} %collective-permute-done.3, bf16[1024,6144]{1,0:T(8,128)(2,1)S(1)} %bitcast.256, s32[]{:T(128)S(6)} %select_n.172), kind=kOutput, calls=%fused_computation.72 | convolution fusion | flops 2415919104 | bytes 10223620 | tf_op jit(solution)/shard_map/td,kdc->ktc/dot_general | solution.py:129
  182.7 6.2 %fusion.37 = f32[1024,3,512]{2,0,1:T(8,128)} fusion(bf16[3,768,512]{2,1,0:T(8,128)(2,1)} %collective-permute-done.2, bf16[1024,6144]{1,0:T(8,128)(2,1)S(1)} %bitcast.256, s32[]{:T(128)S(6)} %select_n.171), kind=kOutput, calls=%fused_computation.75 | convolution fusion | flops 2415919104 | bytes 10223620 | tf_op jit(solution)/shard_map/td,kdc->ktc/dot_general | solution.py:129
  190.3 18.9 %add_bitcast_fusion = f32[3,1024,512]{2,1,0:T(8,128)} fusion(f32[1024,3,512]{2,0,1:T(8,128)} %fusion.31, f32[1024,3,512]{2,0,1:T(8,128)} %fusion.34, f32[1024,3,512]{2,0,1:T(8,128)} %fusion.37, f32[1024,3,512]{2,0,1:T(8,128)} %fusion.40, f32[1024,3,512]{2,0,1:T(8,128)} %fusion.43, f32[1024,3,512]{2,0,1:T(8,128)} %fusion.51, f32[1024,3,512]{2,0,1:T(8,128)} %fusion.47, ...), kind=kOutput, calls=%fused_computation.14 | convolution fusion | flops 2426929152 | bytes 54263812 | tf_op jit(solution)/shard_map/td,kdc->ktc/dot_general | solution.py:129
  227.6 7.3 %while.38 = (s32[]{:T(128)}, f32[4]{0:T(128)S(1)}, f32[4,128,128]{2,1,0:T(8,128)S(1)}, f32[4,4]{1,0:T(4,128)S(1)}, f32[4,4,128,128]{3,2,1,0:T(8,128)}, /*index=5...) while((s32[]{:T(128)}, f32[4]{0:T(128)S(1)}, ...), condition=%wide.region_5.6_spmd.clone, body=%wide.region_4.5_spmd.clone.sunk | while | flops 262155 | bytes 1311477 | solution.py:176
  240.4 7.4 %while.39 = (s32[]{:T(128)}, f32[4]{0:T(128)S(1)}, f32[4,128,128]{2,1,0:T(8,128)S(1)}, f32[4,4]{1,0:T(4,128)S(1)}, f32[4,4,128,128]{3,2,1,0:T(8,128)}, /*index=5...) while((s32[]{:T(128)}, f32[4]{0:T(128)S(1)}, ...), condition=%wide.region_7.8_spmd.clone, body=%wide.region_6.7_spmd.clone.sunk | while | flops 262156 | bytes 1310989 | solution.py:179
  255.9 5.5 %fusion.53 = f32[4,4,256,128]{3,2,1,0:T(8,128)} fusion(f32[4,4,256]{2,1,0:T(4,128)S(1)} %reduce_window_sum.30, pred[4,256,256]{1,2,0:T(8,128)(4,1)S(1)} %copy-done.19, bf16[4,256,4,128]{3,1,0,2:T(8,128)(2,1)S(1)} %multiply_convert_fusion.6, bf16[4,256,4,128]{3,2,1,0:T(4,128)(2,1)} %reshape.196, f32[4,256,4,128]{3,2,1,0:T(4,128)} %squeeze.48), kind=kOutput, calls=%fused_computation.91 | convolution fusion | flops 545259520 | bytes 6569984 | tf_op jit(solution)/shard_map/hbts,hbtf->hbsf/dot_general | solution.py:225
  292.1 5.4 %multiply_convert_fusion.2 = (bf16[1,1024,512]{2,1,0:T(8,128)(2,1)S(1)}, bf16[1,1024,512]{2,1,0:T(8,128)(2,1)}) fusion(f32[1,1024,512]{2,1,0:T(8,128)} %reshape.199, f32[3,1024,512]{2,1,0:T(8,128)} %add_bitcast_fusion, f32[1,1024,512]{2,1,0:T(8,128)S(1)} %copy-done.2), kind=kLoop, calls=%fused_computation.52 | loop fusion | flops 9961472 | bytes 10485760 | tf_op jit(solution)/shard_map/convert.6
  297.5 6.1 %broadcast_in_dim.91 = bf16[1024,6144]{1,0:T(8,128)(2,1)} broadcast(bf16[]{:T(256)} %constant.85.clone.1), dimensions={} | broadcast | bytes 12582914 | tf_op jit(solution)/shard_map/broadcast_in_dim | solution.py:247
  303.6 5.5 %fusion.17 = bf16[1024,6144]{1,0:T(8,128)(2,1)} fusion(bf16[1024,6144]{1,0:T(8,128)(2,1)} %broadcast_in_dim.91, s32[]{:T(128)S(6)} %select_n.167, bf16[3,1536,512]{2,1,0:T(8,128)(2,1)S(1)} %bitcast.252, bf16[1,1024,512]{2,1,0:T(8,128)(2,1)} %stack_reshape.4, bf16[1,1024,512]{2,1,0:T(8,128)(2,1)} %get-tuple-element.341, ...), kind=kOutput, calls=%fused_computation.57 | convolution fusion | flops 2419851264 | bytes 7077892 | tf_op jit(solution)/shard_map/ktc,kdc->td/dot_general | solution.py:249
  313.1 5.5 %fusion.19 = bf16[1024,6144]{1,0:T(8,128)(2,1)} fusion(bf16[1024,6144]{1,0:T(8,128)(2,1)} %fusion.18, s32[]{:T(128)S(6)} %select_n.169, bf16[3,768,512]{2,1,0:T(8,128)(2,1)} %collective-permute-done, bf16[1,1024,512]{2,1,0:T(8,128)(2,1)S(1)} %copy-done.15, bf16[1,1024,512]{2,1,0:T(8,128)(2,1)S(1)} %copy-done.12, ...), kind=kOutput, calls=%fused_computation.59 | convolution fusion | flops 2419851264 | bytes 7077892 | tf_op jit(solution)/shard_map/ktc,kdc->td/dot_general | solution.py:249
  318.5 5.5 %fusion.20 = bf16[1024,6144]{1,0:T(8,128)(2,1)} fusion(bf16[1024,6144]{1,0:T(8,128)(2,1)} %fusion.19, s32[]{:T(128)S(6)} %select_n.170, bf16[3,768,512]{2,1,0:T(8,128)(2,1)} %collective-permute-done.1, bf16[1,1024,512]{2,1,0:T(8,128)(2,1)S(1)} %copy-done.15, bf16[1,1024,512]{2,1,0:T(8,128)(2,1)S(1)} %copy-done.12, ...), kind=kOutput, calls=%fused_computation.60 | convolution fusion | flops 2419851264 | bytes 7077892 | tf_op jit(solution)/shard_map/ktc,kdc->td/dot_general | solution.py:249
  324.0 5.9 %fusion.21 = bf16[1024,6144]{1,0:T(8,128)(2,1)} fusion(bf16[1024,6144]{1,0:T(8,128)(2,1)} %fusion.20, s32[]{:T(128)S(6)} %select_n.171, bf16[3,768,512]{2,1,0:T(8,128)(2,1)} %collective-permute-done.2, bf16[1,1024,512]{2,1,0:T(8,128)(2,1)S(1)} %copy-done.15, bf16[1,1024,512]{2,1,0:T(8,128)(2,1)S(1)} %copy-done.12, ...), kind=kOutput, calls=%fused_computation.61 | convolution fusion | flops 2419851264 | bytes 7077892 | tf_op jit(solution)/shard_map/ktc,kdc->td/dot_general | solution.py:249
  330.0 5.5 %fusion.22 = bf16[1024,6144]{1,0:T(8,128)(2,1)} fusion(bf16[1024,6144]{1,0:T(8,128)(2,1)} %fusion.21, s32[]{:T(128)S(6)} %select_n.172, bf16[3,768,512]{2,1,0:T(8,128)(2,1)} %collective-permute-done.3, bf16[1,1024,512]{2,1,0:T(8,128)(2,1)S(1)} %copy-done.15, bf16[1,1024,512]{2,1,0:T(8,128)(2,1)S(1)} %copy-done.12, ...), kind=kOutput, calls=%fused_computation.62 | convolution fusion | flops 2419851264 | bytes 7077892 | tf_op jit(solution)/shard_map/ktc,kdc->td/dot_general | solution.py:249
  335.5 5.6 %fusion.23 = bf16[1024,6144]{1,0:T(8,128)(2,1)} fusion(bf16[1024,6144]{1,0:T(8,128)(2,1)} %fusion.22, s32[]{:T(128)S(6)} %select_n.173, bf16[3,768,512]{2,1,0:T(8,128)(2,1)} %collective-permute-done.4, bf16[1,1024,512]{2,1,0:T(8,128)(2,1)S(1)} %copy-done.15, bf16[1,1024,512]{2,1,0:T(8,128)(2,1)S(1)} %copy-done.12, ...), kind=kOutput, calls=%fused_computation.63 | convolution fusion | flops 2419851264 | bytes 7077892 | tf_op jit(solution)/shard_map/ktc,kdc->td/dot_general | solution.py:249
  368.1 37.5 %collective-permute-done.10 = bf16[3,768,512]{1,2,0:T(8,128)(2,1)S(1)} collective-permute-done((bf16[3,768,512]{1,2,0:T(8,128)(2,1)S(1)}, bf16[3,768,512]{1,2,0:T(8,128)(2,1)S(1)}, u32[]{:S(2)}, u32[]{:S(2)}) %collective-permute-start.10) | collective-permute-done | bytes 2359328 | tf_op jit(solution)/shard_map/ppermute | solution.py:11
  423.6 32.6 %collective-permute-done.9 = bf16[3,768,512]{1,2,0:T(8,128)(2,1)S(1)} collective-permute-done((bf16[3,768,512]{1,2,0:T(8,128)(2,1)S(1)}, bf16[3,768,512]{1,2,0:T(8,128)(2,1)S(1)}, u32[]{:S(2)}, u32[]{:S(2)}) %collective-permute-start.9) | collective-permute-done | bytes 2359328 | tf_op jit(solution)/shard_map/ppermute | solution.py:11
  456.2 53.3 %collective-permute-done.11 = bf16[3,768,512]{1,2,0:T(8,128)(2,1)S(1)} collective-permute-done((bf16[3,768,512]{1,2,0:T(8,128)(2,1)S(1)}, bf16[3,768,512]{1,2,0:T(8,128)(2,1)S(1)}, u32[]{:S(2)}, u32[]{:S(2)}) %collective-permute-start.11) | collective-permute-done | bytes 2359328 | tf_op jit(solution)/shard_map/ppermute | solution.py:11
  514.1 6.6 %copy.172 = bf16[1536,3,512]{2,0,1:T(8,128)(2,1)} copy(bf16[1536,3,512]{0,2,1:T(8,128)(2,1)} %maximum_bitcast_fusion) | data formatting | bytes 9437184
  (218 shorter events, 165.8 us)
Async XLA Ops:
  7.2 121.9 %all-gather.2.cloned.1.call-start = ((), (), s32[]{:S(2)}) async-start(), calls=%async_computation.1 | async-start | bytes 14155776 | tf_op jit(solution)/shard_map/all_gather | solution.py:120
  7.9 512.8 %reduce-scatter.2.cloned.1.call-start = ((), (), s32[]{:S(2)}) async-start(), calls=%async_computation.2 | async-start | bytes 14155776 | tf_op jit(solution)/shard_map/reduce_scatter | solution.py:255
  8.0 15.8 %copy-start.14 = (bf16[1024,512]{1,0:T(8,128)(2,1)S(1)}, bf16[1024,512]{1,0:T(8,128)(2,1)}, u32[]{:S(2)}) copy-start(bf16[1024,512]{1,0:T(8,128)(2,1)} %param.11) | copy-start | bytes 3145732
  13.3 55.4 %collective-permute-start.1 = (bf16[3,768,512]{2,1,0:T(8,128)(2,1)}, bf16[3,768,512]{2,1,0:T(8,128)(2,1)}, u32[]{:S(2)}, u32[]{:S(2)}) collective-permute-start(bf16[3,768,512]{2,1,0:T(8,128)(2,1)} %get-tuple-element.345), channel_id=1, source_target_pairs={{0,16},{8,24},{16,0},{24,8},{1,17},{9,25},{17,1},{25,9},{2,18},{10... | collective-permute-start | bytes 7077896 | tf_op jit(solution)/shard_map/ppermute | solution.py:11
  16.3 55.4 %collective-permute-start = (bf16[3,768,512]{2,1,0:T(8,128)(2,1)}, bf16[3,768,512]{2,1,0:T(8,128)(2,1)}, u32[]{:S(2)}, u32[]{:S(2)}) collective-permute-start(bf16[3,768,512]{2,1,0:T(8,128)(2,1)} %get-tuple-element.344), channel_id=1, source_target_pairs={{0,8},{8,0},{16,24},{24,16},{1,9},{9,1},{17,25},{25,17},{2,10},{10... | collective-permute-start | bytes 7077896 | tf_op jit(solution)/shard_map/ppermute | solution.py:11
  17.8 158.8 %collective-permute-start.3 = (bf16[3,768,512]{2,1,0:T(8,128)(2,1)}, bf16[3,768,512]{2,1,0:T(8,128)(2,1)}, u32[]{:S(2)}, u32[]{:S(2)}) collective-permute-start(bf16[3,768,512]{2,1,0:T(8,128)(2,1)} %get-tuple-element.344), channel_id=1, source_target_pairs={{0,16},{8,24},{16,0},{24,8},{1,17},{9,25},{17,1},{25,9},{2,18},{10... | collective-permute-start | bytes 7077896 | tf_op jit(solution)/shard_map/ppermute | solution.py:11
  18.3 164.4 %collective-permute-start.2 = (bf16[3,768,512]{2,1,0:T(8,128)(2,1)}, bf16[3,768,512]{2,1,0:T(8,128)(2,1)}, u32[]{:S(2)}, u32[]{:S(2)}) collective-permute-start(bf16[3,768,512]{2,1,0:T(8,128)(2,1)} %get-tuple-element.345), channel_id=1, source_target_pairs={{0,8},{8,0},{16,24},{24,16},{1,9},{9,1},{17,25},{25,17},{2,10},{10... | collective-permute-start | bytes 7077896 | tf_op jit(solution)/shard_map/ppermute | solution.py:11
  68.7 101.8 %collective-permute-start.4 = (bf16[3,768,512]{2,1,0:T(8,128)(2,1)}, bf16[3,768,512]{2,1,0:T(8,128)(2,1)}, u32[]{:S(2)}, u32[]{:S(2)}) collective-permute-start(bf16[3,768,512]{2,1,0:T(8,128)(2,1)} %collective-permute-done.1), channel_id=1, source_target_pairs={{0,8},{8,0},{16,24},{24,16},{1,9},{9,1},{17,25},{25,17},{2,10},{10... | collective-permute-start | bytes 7077896 | tf_op jit(solution)/shard_map/ppermute | solution.py:11
  71.6 117.2 %collective-permute-start.5 = (bf16[3,768,512]{2,1,0:T(8,128)(2,1)}, bf16[3,768,512]{2,1,0:T(8,128)(2,1)S(1)}, u32[]{:S(2)}, u32[]{:S(2)}) collective-permute-start(bf16[3,768,512]{2,1,0:T(8,128)(2,1)} %collective-permute-done), channel_id=1, source_target_pairs={{0,16},{8,24},{16,0},{24,8},{1,17},{9,25},{17,1},{25,9},{2,18},{10... | collective-permute-start | bytes 7077896 | tf_op jit(solution)/shard_map/ppermute | solution.py:11
  129.1 15.1 %slice-start = ((s8[4718592]{0:T(1024)(128)(4,1)}), s8[4194304]{0:T(1024)(128)(4,1)S(1)}, s32[]{:S(2)}) async-start(s8[4718592]{0:T(1024)(128)(4,1)} %bitcast.246), calls=%async_computation.3 | async-start | bytes 8388608
  129.1 15.1 %slice-start.4 = ((s8[12582912]{0:T(1024)(128)(4,1)}), s8[4194304]{0:T(1024)(128)(4,1)S(1)}, s32[]{:S(2)}) async-start(s8[12582912]{0:T(1024)(128)(4,1)} %bitcast.255), calls=%async_computation.7 | async-start | bytes 8388608
  129.1 15.1 %slice-start.5 = ((s8[12582912]{0:T(1024)(128)(4,1)}), s8[4194304]{0:T(1024)(128)(4,1)S(1)}, s32[]{:S(2)}) async-start(s8[12582912]{0:T(1024)(128)(4,1)} %bitcast.255), calls=%async_computation.8 | async-start | bytes 8388608
  248.6 18.2 %collective-permute-start.6 = (bf16[9,128,128]{2,1,0:T(8,128)(2,1)}, bf16[9,128,128]{2,1,0:T(8,128)(2,1)S(1)}, u32[]{:S(2)}, u32[]{:S(2)}) collective-permute-start(bf16[9,128,128]{2,1,0:T(8,128)(2,1)} %pad_maximum_fusion.1), channel_id=1, source_target_pairs={{0,24},{8,16},{16,8},{24,0},{1,25},{9,17},{17,9},{25,1},{2,26},{10... | collective-permute-start | bytes 884744 | tf_op jit(solution)/shard_map/ppermute | solution.py:11
  250.0 16.8 %collective-permute-start.7 = (bf16[9,128,128]{2,1,0:T(8,128)(2,1)}, bf16[9,128,128]{2,1,0:T(8,128)(2,1)S(1)}, u32[]{:S(2)}, u32[]{:S(2)}) collective-permute-start(bf16[9,128,128]{2,1,0:T(8,128)(2,1)} %pad_maximum_fusion.1), channel_id=1, source_target_pairs={{0,16},{8,24},{16,0},{24,8},{1,17},{9,25},{17,1},{25,9},{2,18},{10... | collective-permute-start | bytes 884744 | tf_op jit(solution)/shard_map/ppermute | solution.py:11
  251.6 16.7 %collective-permute-start.8 = (bf16[9,128,128]{2,1,0:T(8,128)(2,1)}, bf16[9,128,128]{2,1,0:T(8,128)(2,1)}, u32[]{:S(2)}, u32[]{:S(2)}) collective-permute-start(bf16[9,128,128]{2,1,0:T(8,128)(2,1)} %pad_maximum_fusion.1), channel_id=1, source_target_pairs={{0,8},{8,0},{16,24},{24,16},{1,9},{9,1},{17,25},{25,17},{2,10},{10... | collective-permute-start | bytes 884744 | tf_op jit(solution)/shard_map/ppermute | solution.py:11
  297.5 43.6 %copy-start.10 = (bf16[1,1024,512]{2,1,0:T(8,128)(2,1)}, bf16[1,1024,512]{2,1,0:T(8,128)(2,1)S(1)}, u32[]{:S(2)}) copy-start(bf16[1,1024,512]{2,1,0:T(8,128)(2,1)S(1)} %get-tuple-element.340) | copy-start | bytes 3145732
  346.8 11.7 %slice-start.7 = ((s8[12582912]{0:T(1024)(128)(4,1)}), s8[4194304]{0:T(1024)(128)(4,1)S(1)}, s32[]{:S(2)}) async-start(s8[12582912]{0:T(1024)(128)(4,1)} %bitcast.257), calls=%async_computation.10 | async-start | bytes 8388608
  346.8 11.7 %slice-start.8 = ((s8[12582912]{0:T(1024)(128)(4,1)}), s8[4194304]{0:T(1024)(128)(4,1)S(1)}, s32[]{:S(2)}) async-start(s8[12582912]{0:T(1024)(128)(4,1)} %bitcast.257), calls=%async_computation.11 | async-start | bytes 8388608
  351.4 54.2 %collective-permute-start.10 = (bf16[3,768,512]{1,2,0:T(8,128)(2,1)S(1)}, bf16[3,768,512]{1,2,0:T(8,128)(2,1)S(1)}, u32[]{:S(2)}, u32[]{:S(2)}) collective-permute-start(bf16[3,768,512]{1,2,0:T(8,128)(2,1)S(1)} %convert_bitcast_fusion.2), channel_id=1, source_target_pairs={{0,8},{8,0},{16,24},{24,16},{1,9},{9,1},{17,25},{25,17},{2,10},{10... | collective-permute-start | bytes 7077896 | tf_op jit(solution)/shard_map/ppermute | solution.py:11
  357.5 54.2 %collective-permute-start.12 = (bf16[3,768,512]{1,2,0:T(8,128)(2,1)S(1)}, bf16[3,768,512]{1,2,0:T(8,128)(2,1)S(1)}, u32[]{:S(2)}, u32[]{:S(2)}) collective-permute-start(bf16[3,768,512]{1,2,0:T(8,128)(2,1)S(1)} %convert_bitcast_fusion.1), channel_id=1, source_target_pairs={{0,16},{8,24},{16,0},{24,8},{1,17},{9,25},{17,1},{25,9},{2,18},{10... | collective-permute-start | bytes 7077896 | tf_op jit(solution)/shard_map/ppermute | solution.py:11
  361.6 94.6 %collective-permute-start.9 = (bf16[3,768,512]{1,2,0:T(8,128)(2,1)S(1)}, bf16[3,768,512]{1,2,0:T(8,128)(2,1)S(1)}, u32[]{:S(2)}, u32[]{:S(2)}) collective-permute-start(bf16[3,768,512]{1,2,0:T(8,128)(2,1)S(1)} %convert_bitcast_fusion.3), channel_id=1, source_target_pairs={{0,8},{8,0},{16,24},{24,16},{1,9},{9,1},{17,25},{25,17},{2,10},{10... | collective-permute-start | bytes 7077896 | tf_op jit(solution)/shard_map/ppermute | solution.py:11
  366.4 144.1 %collective-permute-start.14 = (bf16[3,768,512]{1,2,0:T(8,128)(2,1)}, bf16[3,768,512]{1,2,0:T(8,128)(2,1)S(1)}, u32[]{:S(2)}, u32[]{:S(2)}) collective-permute-start(bf16[3,768,512]{1,2,0:T(8,128)(2,1)} %convert_bitcast_fusion), channel_id=1, source_target_pairs={{0,16},{8,24},{16,0},{24,8},{1,17},{9,25},{17,1},{25,9},{2,18},{10... | collective-permute-start | bytes 7077896 | tf_op jit(solution)/shard_map/ppermute | solution.py:11
  408.7 100.7 %collective-permute-start.11 = (bf16[3,768,512]{1,2,0:T(8,128)(2,1)S(1)}, bf16[3,768,512]{1,2,0:T(8,128)(2,1)S(1)}, u32[]{:S(2)}, u32[]{:S(2)}) collective-permute-start(bf16[3,768,512]{1,2,0:T(8,128)(2,1)S(1)} %fusion.9), channel_id=1, source_target_pairs={{0,16},{8,24},{16,0},{24,8},{1,17},{9,25},{17,1},{25,9},{2,18},{10... | collective-permute-start | bytes 7077896 | tf_op jit(solution)/shard_map/ppermute | solution.py:11
  416.0 94.5 %collective-permute-start.13 = (bf16[3,768,512]{1,2,0:T(8,128)(2,1)}, bf16[3,768,512]{1,2,0:T(8,128)(2,1)S(1)}, u32[]{:S(2)}, u32[]{:S(2)}) collective-permute-start(bf16[3,768,512]{1,2,0:T(8,128)(2,1)} %fusion.6), channel_id=1, source_target_pairs={{0,8},{8,0},{16,24},{24,16},{1,9},{9,1},{17,25},{25,17},{2,10},{10... | collective-permute-start | bytes 7077896 | tf_op jit(solution)/shard_map/ppermute | solution.py:11
  (25 other events, 112.5 us)
Sparse Core Ops, SparseCore 0:
  9.6 119.4 all-gather.1
  345.1 129.5 reduce-scatter.1
where the time goes:
time: 538 us; the launch traced here: 528 us
  waiting for transfers between devices  241 us (45%)
  matrix products  160 us (30%)
  local copies, waits for them, and re-layouts  55.6 us (10%)
  other arithmetic  37.3 us (7%)
  starting transfers between devices  18.8 us (3%)
  between operations  14.7 us (3%)
    ppermute x15, waiting for transfers between devices, hop(): lax.ppermute(array, axis, [(i, i ^ flip) for i in range(lax.axis_size(axi...  184 us
    dot_general x8, matrix products, body(): jnp.einsum('td,kdc->ktc', feature_rows(owner, first, block.shape[1]), blo...  61.6 us
    all_gather x1, waiting for transfers between devices, body(): features = lax.all_gather(inputs, 'head', axis=1, tiled=True)  55.9 us
    dot_general x8, matrix products, body(): jnp.einsum('ktc,kdc->td', project_gradient, block, preferred_element_type...  41.3 us
    dot_general x8, matrix products, weight_partial(): jnp.einsum('td,ktc->kdc', feature_rows(owner, first, count), project_grad...  29.8 us
    ppermute x15, starting transfers between devices, hop(): lax.ppermute(array, axis, [(i, i ^ flip) for i in range(lax.axis_size(axi...  18.7 us
    unnamed x66, local copies, waits for them, and re-layouts  12 us
  transfers between devices with their start and end apart: 17, of which 7 were waited for; matrix products, arithmetic and copies ran while one was open for 22% of the time, Pallas kernels for 0%

commit v1 on v0

--- a/solution.py
+++ b/solution.py
@@ -5,6 +5,30 @@
 
 HEAD_DIM = 128
 BLOCK = 256
+
+
+def _balance_local_data(patch, array_axis):
+    patch = jnp.moveaxis(patch, 0, array_axis)
+    item_now = patch.shape
+    h_now = patch.reshape(
+        *item_now[:array_axis],
+        item_now[array_axis] * item_now[array_axis + 1],
+        *item_now[array_axis + 2 :]
+    )
+    return h_now
+
+
+def number_cells(tile_in, axis_id):
+    full_n = lax.axis_size(axis_id)
+    raw_out = tile_in[None]
+    for rr in range(full_n.bit_length() - 1):
+        n_now = 1 << rr
+        block_next = lax.ppermute(raw_out, axis_id, [(dev, dev ^ n_now) for dev in range(full_n)])
+        block_now = jnp.stack([raw_out, block_next])
+        then = lax.axis_index(axis_id)
+        shaped = then >> rr & 1
+        raw_out = jnp.where(shaped == 0, block_now, block_now[::-1]).reshape(-1, *tile_in.shape)
+    return raw_out
 
 
 def hop(array, axis, flip):
@@ -117,7 +141,8 @@
     local_cols = cotangent.shape[1]
     blocks = tokens // BLOCK
     query_scale = HEAD_DIM ** (-0.5)
-    features = lax.all_gather(inputs, "head", axis=1, tiled=True)
+    y2 = number_cells(inputs, "head")
+    features = _balance_local_data(y2, 1)
     rows = projection.shape[0]
     blocks_w = gather_rows(projection.transpose(1, 0, 2), "seq")
 

time: 538 us -> 759 us (1.41)
  waiting for transfers between devices: 241 us -> 448 us
  other arithmetic: 37.3 us -> 57.6 us
    ppermute x0 -> x3, waiting for transfers between devices: none -> 233 us  [number_cells(): lax.ppermute(raw_out, axis_id, [(dev, dev ^ n_now) for dev in range(full_...]
    all_gather x1 -> x0, waiting for transfers between devices: 55.9 us -> none  [body(): features = lax.all_gather(inputs, 'head', axis=1, tiled=True)]
    ppermute x15, waiting for transfers between devices: 184 us -> 214 us  [hop(): lax.ppermute(array, axis, [(i, i ^ flip) for i in range(lax.axis_size(axi...]
    another operation x4 -> x8, other arithmetic: 10.3 us -> 23.4 us  [the longest x4 12.9 us: number_cells(): block_now = jnp.stack([raw_out, block_next])]
  transfers between devices with their start and end apart: 17 -> 19, of which waited for: 7 -> 8; matrix products, arithmetic and copies ran while one was open for 22% -> 16% of each run, Pallas kernels for 0% -> 0%
where the time goes in v1:
time: 759 us; the launch traced here: 754 us
  waiting for transfers between devices  448 us (59%)
  matrix products  155 us (20%)
  other arithmetic  57.6 us (8%)
  local copies, waits for them, and re-layouts  55.1 us (7%)
  starting transfers between devices  23.9 us (3%)
  between operations  14.8 us (2%)
    ppermute x3, waiting for transfers between devices, number_cells(): lax.ppermute(raw_out, axis_id, [(dev, dev ^ n_now) for dev in range(full_...  233 us
    ppermute x15, waiting for transfers between devices, hop(): lax.ppermute(array, axis, [(i, i ^ flip) for i in range(lax.axis_size(axi...  214 us
    dot_general x8, matrix products, body(): jnp.einsum('td,kdc->ktc', feature_rows(owner, first, block.shape[1]), blo...  57.9 us
    dot_general x8, matrix products, body(): jnp.einsum('ktc,kdc->td', project_gradient, block, preferred_element_type...  39.4 us
    dot_general x8, matrix products, weight_partial(): jnp.einsum('td,ktc->kdc', feature_rows(owner, first, count), project_grad...  30.4 us
    ppermute x15, starting transfers between devices, hop(): lax.ppermute(array, axis, [(i, i ^ flip) for i in range(lax.axis_size(axi...  17.6 us
  transfers between devices with their start and end apart: 19, of which 8 were waited for; matrix products, arithmetic and copies ran while one was open for 16% of the time, Pallas kernels for 0%

profile of v1, /device:TPU:0, one launch (start us, length us, event | category | flops | bytes accessed | tf_op | source)
XLA Modules:
  0.0 754.3 jit_solution(4688926568974932525)
XLA Ops:
  18.0 68.7 %collective-permute-done.1 = bf16[2,1024,768]{2,1,0:T(8,128)(2,1)} collective-permute-done((bf16[2,1024,768]{2,1,0:T(8,128)(2,1)}, bf16[2,1024,768]{2,1,0:T(8,128)(2,1)}, u32[]{:S(2)}, u32[]{:S(2)}) %collective-permute-start.1) | collective-permute-done | bytes 3145760 | tf_op jit(solution)/shard_map/ppermute | solution.py:26
  113.2 90.1 %collective-permute-done.4 = bf16[3,768,512]{2,1,0:T(8,128)(2,1)} collective-permute-done((bf16[3,768,512]{2,1,0:T(8,128)(2,1)}, bf16[3,768,512]{2,1,0:T(8,128)(2,1)}, u32[]{:S(2)}, u32[]{:S(2)}) %collective-permute-start.4) | collective-permute-done | bytes 2359328 | tf_op jit(solution)/shard_map/ppermute | solution.py:35
  205.3 161.1 %collective-permute-done.2 = bf16[4,1024,768]{2,1,0:T(8,128)(2,1)} collective-permute-done((bf16[4,1024,768]{2,1,0:T(8,128)(2,1)}, bf16[4,1024,768]{2,1,0:T(8,128)(2,1)}, u32[]{:S(2)}, u32[]{:S(2)}) %collective-permute-start.2) | collective-permute-done | bytes 6291488 | tf_op jit(solution)/shard_map/ppermute | solution.py:26
  366.5 6.2 pad_maximum_fusion
  377.9 5.3 fusion.49
  387.7 6.1 fusion.45
  393.9 6.2 fusion.42
  400.1 6.1 fusion.36
  410.7 6.2 fusion.39
  418.2 19.0 %add_bitcast_fusion = f32[3,1024,512]{2,1,0:T(8,128)} fusion(f32[1024,3,512]{2,0,1:T(8,128)} %fusion.33, f32[1024,3,512]{2,0,1:T(8,128)} %fusion.36, f32[1024,3,512]{2,0,1:T(8,128)} %fusion.39, f32[1024,3,512]{2,0,1:T(8,128)} %fusion.42, f32[1024,3,512]{2,0,1:T(8,128)} %fusion.45, f32[1024,3,512]{2,0,1:T(8,128)} %fusion.53, f32[1024,3,512]{2,0,1:T(8,128)} %fusion.49, ...), kind=kOutput, calls=%fused_computation.18 | convolution fusion | flops 2426929152 | bytes 54263812 | tf_op jit(solution)/shard_map/td,kdc->ktc/dot_general | solution.py:154
  455.6 7.3 while.38
  468.5 7.4 while.39
  484.1 5.4 fusion.55
  520.3 5.4 multiply_convert_fusion.2
  525.7 6.1 broadcast_in_dim.94
  531.8 5.6 fusion.19
  541.3 5.5 fusion.21
  546.8 5.5 fusion.22
  552.3 5.6 fusion.23
  557.9 5.6 fusion.24
  594.1 37.8 %collective-permute-done.13 = bf16[3,768,512]{1,2,0:T(8,128)(2,1)S(1)} collective-permute-done((bf16[3,768,512]{1,2,0:T(8,128)(2,1)S(1)}, bf16[3,768,512]{1,2,0:T(8,128)(2,1)S(1)}, u32[]{:S(2)}, u32[]{:S(2)}) %collective-permute-start.13) | collective-permute-done | bytes 2359328 | tf_op jit(solution)/shard_map/ppermute | solution.py:35
  650.5 32.1 %collective-permute-done.12 = bf16[3,768,512]{1,2,0:T(8,128)(2,1)S(1)} collective-permute-done((bf16[3,768,512]{1,2,0:T(8,128)(2,1)S(1)}, bf16[3,768,512]{1,2,0:T(8,128)(2,1)S(1)}, u32[]{:S(2)}, u32[]{:S(2)}) %collective-permute-start.12) | collective-permute-done | bytes 2359328 | tf_op jit(solution)/shard_map/ppermute | solution.py:35
  682.5 53.6 %collective-permute-done.14 = bf16[3,768,512]{1,2,0:T(8,128)(2,1)S(1)} collective-permute-done((bf16[3,768,512]{1,2,0:T(8,128)(2,1)}, bf16[3,768,512]{1,2,0:T(8,128)(2,1)S(1)}, u32[]{:S(2)}, u32[]{:S(2)}) %collective-permute-start.14) | collective-permute-done | bytes 2359328 | tf_op jit(solution)/shard_map/ppermute | solution.py:35
  740.6 6.6 copy.176
  (232 shorter events, 189.6 us)
Async XLA Ops:
  7.2 740.0 %reduce-scatter.2.cloned.1.call-start = ((), (), s32[]{:S(2)}) async-start(), calls=%async_computation.1 | async-start | bytes 14155776 | tf_op jit(solution)/shard_map/reduce_scatter | solution.py:280
  7.2 3.8 collective-permute-start
  15.1 71.7 %collective-permute-start.1 = (bf16[2,1024,768]{2,1,0:T(8,128)(2,1)}, bf16[2,1024,768]{2,1,0:T(8,128)(2,1)}, u32[]{:S(2)}, u32[]{:S(2)}) collective-permute-start(bf16[2,1024,768]{2,1,0:T(8,128)(2,1)} %get-tuple-element.347), channel_id=1, source_target_pairs={{0,2},{1,3},{2,0},{3,1},{4,6},{5,7},{6,4},{7,5},{8,10},{9,11},{10,... | collective-permute-start | bytes 9437192 | tf_op jit(solution)/shard_map/ppermute | solution.py:26
  93.4 273.1 %collective-permute-start.2 = (bf16[4,1024,768]{2,1,0:T(8,128)(2,1)}, bf16[4,1024,768]{2,1,0:T(8,128)(2,1)}, u32[]{:S(2)}, u32[]{:S(2)}) collective-permute-start(bf16[4,1024,768]{2,1,0:T(8,128)(2,1)} %bitcast.7), channel_id=1, source_target_pairs={{0,4},{1,5},{2,6},{3,7},{4,0},{5,1},{6,2},{7,3},{8,12},{9,13},{10,... | collective-permute-start | bytes 18874376 | tf_op jit(solution)/shard_map/ppermute | solution.py:26
  96.2 12.5 %copy-start.15 = (bf16[1024,512]{1,0:T(8,128)(2,1)S(1)}, bf16[1024,512]{1,0:T(8,128)(2,1)}, u32[]{:S(2)}) copy-start(bf16[1024,512]{1,0:T(8,128)(2,1)} %param.11) | copy-start | bytes 3145732
  99.0 104.8 %collective-permute-start.3 = (bf16[3,768,512]{2,1,0:T(8,128)(2,1)}, bf16[3,768,512]{2,1,0:T(8,128)(2,1)}, u32[]{:S(2)}, u32[]{:S(2)}) collective-permute-start(bf16[3,768,512]{2,1,0:T(8,128)(2,1)} %get-tuple-element.344), channel_id=1, source_target_pairs={{0,8},{8,0},{16,24},{24,16},{1,9},{9,1},{17,25},{25,17},{2,10},{10... | collective-permute-start | bytes 7077896 | tf_op jit(solution)/shard_map/ppermute | solution.py:35
  100.5 299.6 %collective-permute-start.6 = (bf16[3,768,512]{2,1,0:T(8,128)(2,1)}, bf16[3,768,512]{2,1,0:T(8,128)(2,1)}, u32[]{:S(2)}, u32[]{:S(2)}) collective-permute-start(bf16[3,768,512]{2,1,0:T(8,128)(2,1)} %get-tuple-element.344), channel_id=1, source_target_pairs={{0,16},{8,24},{16,0},{24,8},{1,17},{9,25},{17,1},{25,9},{2,18},{10... | collective-permute-start | bytes 7077896 | tf_op jit(solution)/shard_map/ppermute | solution.py:35
  102.0 101.3 %collective-permute-start.4 = (bf16[3,768,512]{2,1,0:T(8,128)(2,1)}, bf16[3,768,512]{2,1,0:T(8,128)(2,1)}, u32[]{:S(2)}, u32[]{:S(2)}) collective-permute-start(bf16[3,768,512]{2,1,0:T(8,128)(2,1)} %get-tuple-element.345), channel_id=1, source_target_pairs={{0,16},{8,24},{16,0},{24,8},{1,17},{9,25},{17,1},{25,9},{2,18},{10... | collective-permute-start | bytes 7077896 | tf_op jit(solution)/shard_map/ppermute | solution.py:35
  102.5 308.1 %collective-permute-start.5 = (bf16[3,768,512]{2,1,0:T(8,128)(2,1)}, bf16[3,768,512]{2,1,0:T(8,128)(2,1)}, u32[]{:S(2)}, u32[]{:S(2)}) collective-permute-start(bf16[3,768,512]{2,1,0:T(8,128)(2,1)} %get-tuple-element.345), channel_id=1, source_target_pairs={{0,8},{8,0},{16,24},{24,16},{1,9},{9,1},{17,25},{25,17},{2,10},{10... | collective-permute-start | bytes 7077896 | tf_op jit(solution)/shard_map/ppermute | solution.py:35
  203.3 202.9 %collective-permute-start.7 = (bf16[3,768,512]{2,1,0:T(8,128)(2,1)}, bf16[3,768,512]{2,1,0:T(8,128)(2,1)S(1)}, u32[]{:S(2)}, u32[]{:S(2)}) collective-permute-start(bf16[3,768,512]{2,1,0:T(8,128)(2,1)} %collective-permute-done.4), channel_id=1, source_target_pairs={{0,8},{8,0},{16,24},{24,16},{1,9},{9,1},{17,25},{25,17},{2,10},{10... | collective-permute-start | bytes 7077896 | tf_op jit(solution)/shard_map/ppermute | solution.py:35
  203.8 213.0 %collective-permute-start.8 = (bf16[3,768,512]{2,1,0:T(8,128)(2,1)}, bf16[3,768,512]{2,1,0:T(8,128)(2,1)S(1)}, u32[]{:S(2)}, u32[]{:S(2)}) collective-permute-start(bf16[3,768,512]{2,1,0:T(8,128)(2,1)} %collective-permute-done.3), channel_id=1, source_target_pairs={{0,16},{8,24},{16,0},{24,8},{1,17},{9,25},{17,1},{25,9},{2,18},{10... | collective-permute-start | bytes 7077896 | tf_op jit(solution)/shard_map/ppermute | solution.py:35
  377.8 32.8 %copy-start = (bf16[128,8,8,768]{3,1,2,0:T(8,128)(2,1)}, bf16[128,8,8,768]{3,1,2,0:T(8,128)(2,1)S(1)}, u32[]{:S(2)}) copy-start(bf16[128,8,8,768]{3,1,2,0:T(8,128)(2,1)S(1)} %copy.193) | copy-start | bytes 37748740
  476.7 18.3 %collective-permute-start.10 = (bf16[9,128,128]{2,1,0:T(8,128)(2,1)}, bf16[9,128,128]{2,1,0:T(8,128)(2,1)S(1)}, u32[]{:S(2)}, u32[]{:S(2)}) collective-permute-start(bf16[9,128,128]{2,1,0:T(8,128)(2,1)} %pad_maximum_fusion.4), channel_id=1, source_target_pairs={{0,16},{8,24},{16,0},{24,8},{1,17},{9,25},{17,1},{25,9},{2,18},{10... | collective-permute-start | bytes 884744 | tf_op jit(solution)/shard_map/ppermute | solution.py:35
  478.1 16.9 %collective-permute-start.11 = (bf16[9,128,128]{2,1,0:T(8,128)(2,1)}, bf16[9,128,128]{2,1,0:T(8,128)(2,1)S(1)}, u32[]{:S(2)}, u32[]{:S(2)}) collective-permute-start(bf16[9,128,128]{2,1,0:T(8,128)(2,1)} %pad_maximum_fusion.4), channel_id=1, source_target_pairs={{0,8},{8,0},{16,24},{24,16},{1,9},{9,1},{17,25},{25,17},{2,10},{10... | collective-permute-start | bytes 884744 | tf_op jit(solution)/shard_map/ppermute | solution.py:35
  479.5 16.9 %collective-permute-start.9 = (bf16[9,128,128]{2,1,0:T(8,128)(2,1)}, bf16[9,128,128]{2,1,0:T(8,128)(2,1)}, u32[]{:S(2)}, u32[]{:S(2)}) collective-permute-start(bf16[9,128,128]{2,1,0:T(8,128)(2,1)} %pad_maximum_fusion.4), channel_id=1, source_target_pairs={{0,24},{8,16},{16,8},{24,0},{1,25},{9,17},{17,9},{25,1},{2,26},{10... | collective-permute-start | bytes 884744 | tf_op jit(solution)/shard_map/ppermute | solution.py:35
  525.7 41.7 %copy-start.11 = (bf16[1,1024,512]{2,1,0:T(8,128)(2,1)}, bf16[1,1024,512]{2,1,0:T(8,128)(2,1)S(1)}, u32[]{:S(2)}) copy-start(bf16[1,1024,512]{2,1,0:T(8,128)(2,1)S(1)} %get-tuple-element.340) | copy-start | bytes 3145732
  573.1 12.9 %slice-start = ((s8[12582912]{0:T(1024)(128)(4,1)}), s8[4194304]{0:T(1024)(128)(4,1)S(1)}, s32[]{:S(2)}) async-start(s8[12582912]{0:T(1024)(128)(4,1)} %bitcast.272), calls=%async_computation.2 | async-start | bytes 8388608
  573.2 12.9 %slice-start.1 = ((s8[12582912]{0:T(1024)(128)(4,1)}), s8[4194304]{0:T(1024)(128)(4,1)S(1)}, s32[]{:S(2)}) async-start(s8[12582912]{0:T(1024)(128)(4,1)} %bitcast.272), calls=%async_computation.3 | async-start | bytes 8388608
  577.7 54.3 %collective-permute-start.13 = (bf16[3,768,512]{1,2,0:T(8,128)(2,1)S(1)}, bf16[3,768,512]{1,2,0:T(8,128)(2,1)S(1)}, u32[]{:S(2)}, u32[]{:S(2)}) collective-permute-start(bf16[3,768,512]{1,2,0:T(8,128)(2,1)S(1)} %convert_bitcast_fusion.2), channel_id=1, source_target_pairs={{0,8},{8,0},{16,24},{24,16},{1,9},{9,1},{17,25},{25,17},{2,10},{10... | collective-permute-start | bytes 7077896 | tf_op jit(solution)/shard_map/ppermute | solution.py:35
  584.2 54.3 %collective-permute-start.15 = (bf16[3,768,512]{1,2,0:T(8,128)(2,1)S(1)}, bf16[3,768,512]{1,2,0:T(8,128)(2,1)S(1)}, u32[]{:S(2)}, u32[]{:S(2)}) collective-permute-start(bf16[3,768,512]{1,2,0:T(8,128)(2,1)S(1)} %convert_bitcast_fusion.1), channel_id=1, source_target_pairs={{0,16},{8,24},{16,0},{24,8},{1,17},{9,25},{17,1},{25,9},{2,18},{10... | collective-permute-start | bytes 7077896 | tf_op jit(solution)/shard_map/ppermute | solution.py:35
  589.2 93.4 %collective-permute-start.12 = (bf16[3,768,512]{1,2,0:T(8,128)(2,1)S(1)}, bf16[3,768,512]{1,2,0:T(8,128)(2,1)S(1)}, u32[]{:S(2)}, u32[]{:S(2)}) collective-permute-start(bf16[3,768,512]{1,2,0:T(8,128)(2,1)S(1)} %convert_bitcast_fusion.3), channel_id=1, source_target_pairs={{0,8},{8,0},{16,24},{24,16},{1,9},{9,1},{17,25},{25,17},{2,10},{10... | collective-permute-start | bytes 7077896 | tf_op jit(solution)/shard_map/ppermute | solution.py:35
  593.5 143.6 %collective-permute-start.17 = (bf16[3,768,512]{1,2,0:T(8,128)(2,1)S(1)}, bf16[3,768,512]{1,2,0:T(8,128)(2,1)S(1)}, u32[]{:S(2)}, u32[]{:S(2)}) collective-permute-start(bf16[3,768,512]{1,2,0:T(8,128)(2,1)S(1)} %convert_bitcast_fusion), channel_id=1, source_target_pairs={{0,16},{8,24},{16,0},{24,8},{1,17},{9,25},{17,1},{25,9},{2,18},{10... | collective-permute-start | bytes 7077896 | tf_op jit(solution)/shard_map/ppermute | solution.py:35
  636.1 100.0 %collective-permute-start.14 = (bf16[3,768,512]{1,2,0:T(8,128)(2,1)}, bf16[3,768,512]{1,2,0:T(8,128)(2,1)S(1)}, u32[]{:S(2)}, u32[]{:S(2)}) collective-permute-start(bf16[3,768,512]{1,2,0:T(8,128)(2,1)} %fusion.9), channel_id=1, source_target_pairs={{0,16},{8,24},{16,0},{24,8},{1,17},{9,25},{17,1},{25,9},{2,18},{10... | collective-permute-start | bytes 7077896 | tf_op jit(solution)/shard_map/ppermute | solution.py:35
  642.8 94.2 %collective-permute-start.16 = (bf16[3,768,512]{1,2,0:T(8,128)(2,1)}, bf16[3,768,512]{1,2,0:T(8,128)(2,1)S(1)}, u32[]{:S(2)}, u32[]{:S(2)}) collective-permute-start(bf16[3,768,512]{1,2,0:T(8,128)(2,1)} %fusion.6), channel_id=1, source_target_pairs={{0,8},{8,0},{16,24},{24,16},{1,9},{9,1},{17,25},{25,17},{2,10},{10... | collective-permute-start | bytes 7077896 | tf_op jit(solution)/shard_map/ppermute | solution.py:35
  (29 other events, 123.8 us)
Sparse Core Ops, SparseCore 0:
  571.4 130.1 reduce-scatter.1
